TPU v7x, 32 devices: a whole 2x2x4 slice. The times are simulated.
32 devices in a mesh: space: 8 (over z, y), band: 4 (over x, core).
Axes of the slice: x: 2, y: 2, z: 4, core: 2. Of those that a mesh axis runs over, the one named last changes fastest.
Arguments:
- columns: float32 [16, 48, 32, 128], P('band', 'space'), may hold values from -6 to 6
- potential: float32 [48, 32, 128], P('space'), may hold values from -1 to 3
- orbitals: float32 [512, 48, 32, 128], P('band', 'space'), may hold values from -0.0546875 to 0.0546875
Outputs:
- projected: float32 [16, 48, 32, 128], P('band', 'space')
- correlation: float32 [512, 16], P('band')
All inputs are finite; a program needn't handle non-finite values.
Results may differ from a plain program's by a relative error of at most 0.00011.
Values sent between devices are 32-bit elements; how exact they have to be, the bound alone decides.
No kernel may reach another device: no remote copies, remote signals or barrier semaphores. Data moves between devices by JAX's collectives and lax.ppermute only.
A program may use at most 128 MiB of HBM per device.

v0:
```python
import jax
import jax.numpy as jnp
from jax import lax
from jax.sharding import PartitionSpec as P

COEFFS = (
    -5369.0 / 1800.0,
    12.0 / 7.0,
    -15.0 / 56.0,
    10.0 / 189.0,
    -1.0 / 112.0,
    2.0 / 1925.0,
    -1.0 / 16632.0,
)


def padded_2(array, sides, width):
    for axis, dim in sides:
        size, length = (lax.axis_size(axis), array.shape[dim])
        up = [(i, (i + 1) % size) for i in range(size)]
        down = [(j, i) for i, j in up]
        last = lax.slice_in_dim(array, length - width, length, axis=dim)
        first = lax.slice_in_dim(array, 0, width, axis=dim)
        before = lax.ppermute(last, axis, up)
        after = lax.ppermute(first, axis, down)
        array = jnp.concatenate([before, array, after], axis=dim)
    return array


def hamiltonian(values, potential):
    padded = padded_2(values, (("space", 1),), 6)
    planes = values.shape[1]
    laplace = 3.0 * COEFFS[0] * values
    for offset in range(1, 7):
        along = (
            padded[:, 6 + offset : 6 + offset + planes]
            + padded[:, 6 - offset : 6 - offset + planes]
        )
        along = along + jnp.roll(values, offset, 2) + jnp.roll(values, -offset, 2)
        along = along + jnp.roll(values, offset, 3) + jnp.roll(values, -offset, 3)
        laplace = laplace + COEFFS[offset] * along
    return -0.5 * laplace + potential[None] * values


def shards(columns, potential, orbitals):
    applied = hamiltonian(columns, potential)
    orb_local = orbitals.shape[0]
    col_local = applied.shape[0]
    psi_flat = orbitals.reshape(orb_local, -1)
    piece = lax.all_gather(applied, "band", axis=0, tiled=True)
    partial_correlation = jnp.einsum(
        "oc,kc->ok", psi_flat, piece.reshape(piece.shape[0], -1), precision=lax.Precision.HIGHEST
    )
    correlation = lax.psum(partial_correlation, "space")
    removed = jnp.einsum("ok,oc->kc", correlation, psi_flat, precision=lax.Precision.HIGHEST)
    removed_all = lax.psum_scatter(
        removed.reshape((col_local * lax.axis_size("band"),) + applied.shape[1:]),
        "band",
        scatter_dimension=0,
        tiled=True,
    )
    projected = applied - removed_all
    return (projected, correlation)


def solution(mesh):
    placed = (
        P("band", "space", None, None),
        P("space", None, None),
        P("band", "space", None, None),
    )
    return jax.shard_map(
        shards,
        mesh=mesh,
        in_specs=placed,
        out_specs=(P("band", "space", None, None), P("band", None)),
        check_vma=False,
    )
```

profile of v0, /device:TPU:0, one launch (start us, length us, event | category | flops | bytes accessed | tf_op | source)
XLA Modules:
  0.0 155.2 jit_solution(5152359355266835999)
XLA Ops:
  7.2 3.0 %collective-permute-start.1 = (f32[4,6,32,128]{3,2,1,0:T(8,128)}, f32[4,6,32,128]{3,2,1,0:T(8,128)S(1)}, u32[]{:S(2)}, u32[]{:S(2)}) collective-permute-start(f32[4,6,32,128]{3,2,1,0:T(8,128)} %param.3), channel_id=1, source_target_pairs={{0,4},{4,8},{8,12},{12,16},{16,20},{20,24},{24,28},{28,0},{1,5},{5... | collective-permute-start | bytes 1179656 | tf_op jit(solution)/shard_map/ppermute | solution.py:24
  10.3 3.1 %collective-permute-start = (f32[4,6,32,128]{3,2,1,0:T(8,128)}, f32[4,6,32,128]{3,2,1,0:T(8,128)S(1)}, u32[]{:S(2)}, u32[]{:S(2)}) collective-permute-start(f32[4,6,32,128]{3,2,1,0:T(8,128)} %param.3), channel_id=1, source_target_pairs={{4,0},{8,4},{12,8},{16,12},{20,16},{24,20},{28,24},{0,28},{5,1},{9... | collective-permute-start | bytes 1179656 | tf_op jit(solution)/shard_map/ppermute | solution.py:25
  13.4 1.3 fusion.69
  14.6 1.4 fusion.67
  16.0 1.4 fusion.68
  17.4 1.3 fusion.65
  18.6 1.4 fusion.63
  20.0 1.4 fusion.64
  21.4 1.3 fusion.61
  22.6 1.0 fusion.62
  23.6 1.4 fusion.59
  25.0 0.2 fusion.60
  25.2 0.1 fusion.57
  25.3 0.2 fusion.55
  25.4 0.2 fusion.56
  25.7 0.2 fusion.51
  25.9 0.2 fusion.52
  26.2 0.2 fusion.47
  26.4 0.2 fusion.48
  26.6 0.8 collective-permute-done.1
  27.4 0.1 constant_dynamic-update-slice_fusion.1
  27.5 2.0 %collective-permute-done = f32[4,6,32,128]{3,2,1,0:T(8,128)S(1)} collective-permute-done((f32[4,6,32,128]{3,2,1,0:T(8,128)}, f32[4,6,32,128]{3,2,1,0:T(8,128)S(1)}, u32[]{:S(2)}, u32[]{:S(2)}) %collective-permute-start) | collective-permute-done | bytes 393248 | tf_op jit(solution)/shard_map/ppermute | solution.py:25
  29.5 3.8 %fusion.16 = f32[4,6,32,128]{3,2,1,0:T(8,128)} fusion(f32[4,12,32,128]{3,2,1,0:T(8,128)S(1)} %get-tuple-element.53, f32[4,12,32,128]{3,2,1,0:T(8,128)S(1)} %constant_dynamic-update-slice_fusion, f32[4,6,31,128]{3,2,1,0:T(8,128)S(1)} %get-tuple-element.49, f32[4,6,1,128]{3,2,1,0:T(1,128)S(1)} %get-tuple-element.51, ...), kind=kLoop, calls=%fused_computation.14 | loop fusion | flops 6881280 | bytes 15040512 | tf_op jit(solution)/shard_map/add | solution.py:42
  33.3 0.2 reduce-scatter.2.cloned.1.call-start
  33.6 18.9 %copy.78 = f32[16,8,192,128]{3,1,2,0:T(8,128)} copy(f32[16,8,192,128]{3,2,1,0:T(8,128)} %bitcast.21) | data formatting | bytes 25165824
  52.5 12.6 %copy.64 = f32[24576,128]{1,0:T(8,128)} copy(f32[24576,128]{0,1:T(8,128)} %bitcast.23) | data formatting | bytes 25165824 | tf_op jit(solution)/shard_map/ok,oc->kc/dot_general | solution.py:55
  65.1 20.7 %fusion.3 = f32[128,16]{0,1:T(8,128)S(1)} fusion(f32[128,6,32,128]{3,2,1,0:T(8,128)} %param.5, f32[16,6,32,128]{3,2,1,0:T(8,128)} %all-gather.2.cloned.1.call-done), kind=kOutput, calls=%fused_computation.4 | convolution fusion | flops 603979776 | bytes 14163968 | tf_op jit(solution)/shard_map/oc,kc->ok/dot_general | solution.py:51
  85.8 21.0 %psum.7 = f32[128,16]{0,1:T(8,128)S(1)} all-reduce(f32[128,16]{0,1:T(8,128)S(1)} %fusion.3), channel_id=1, replica_groups=mesh['space'=8,'band'=4] {'space'}, use_global_device_ids=true, to_apply=%region_0.1 | all-reduce | flops 2048 | bytes 16384 | tf_op jit(solution)/shard_map/psum | solution.py:54
  106.7 12.7 %fusion.45 = f32[16,6,32,128]{3,0,2,1:T(8,128)S(1)} fusion(f32[6,32,128,128]{3,2,1,0:T(8,128)} %bitcast.22, f32[128,16]{0,1:T(8,128)S(1)} %psum.7), kind=kOutput, calls=%fused_computation.52 | convolution fusion | flops 603979776 | bytes 14163968 | tf_op jit(solution)/shard_map/ok,oc->kc/dot_general | solution.py:55
  119.5 1.7 %copy.65 = f32[16,6,32,128]{3,2,1,0:T(8,128)} copy(f32[16,6,32,128]{3,0,2,1:T(8,128)S(1)} %fusion.45) | data formatting | bytes 3145728 | tf_op jit(solution)/shard_map/ok,oc->kc/dot_general | solution.py:55
  121.2 25.4 %reduce-scatter.2.cloned.1.call-done = f32[4,6,32,128]{3,2,1,0:T(8,128)} async-done(((f32[16,6,32,128]{3,2,1,0:T(8,128)}), f32[4,6,32,128]{3,2,1,0:T(8,128)}) %reduce-scatter.2.cloned.1.call-update) | async-done | bytes 393232 | tf_op jit(solution)/shard_map/reduce_scatter | solution.py:56
  146.6 1.8 %sub.3 = f32[4,6,32,128]{3,2,1,0:T(8,128)} subtract(f32[4,6,32,128]{3,2,1,0:T(8,128)S(1)} %copy-done.1, f32[4,6,32,128]{3,2,1,0:T(8,128)} %reduce-scatter.2.cloned.1.call-done) | non-fusion elementwise | flops 98304 | bytes 1179648 | tf_op jit(solution)/shard_map/sub | solution.py:62
  (21 shorter events, 0.4 us)
Async XLA Ops:
  7.2 17.8 %copy-start = (f32[4,6,32,128]{3,2,1,0:T(8,128)S(1)}, f32[4,6,32,128]{3,2,1,0:T(8,128)}, u32[]{:S(2)}) copy-start(f32[4,6,32,128]{3,2,1,0:T(8,128)} %param.3) | copy-start | bytes 1179652
  7.2 57.9 %all-gather.2.cloned.1.call-start = ((), (), s32[]{:S(2)}) async-start(), calls=%async_computation.1 | async-start | bytes 1966080 | tf_op jit(solution)/shard_map/all_gather | solution.py:50
  7.2 20.2 %collective-permute-start.1 = (f32[4,6,32,128]{3,2,1,0:T(8,128)}, f32[4,6,32,128]{3,2,1,0:T(8,128)S(1)}, u32[]{:S(2)}, u32[]{:S(2)}) collective-permute-start(f32[4,6,32,128]{3,2,1,0:T(8,128)} %param.3), channel_id=1, source_target_pairs={{0,4},{4,8},{8,12},{12,16},{16,20},{20,24},{24,28},{28,0},{1,5},{5... | collective-permute-start | bytes 1179656 | tf_op jit(solution)/shard_map/ppermute | solution.py:24
  10.3 19.2 %collective-permute-start = (f32[4,6,32,128]{3,2,1,0:T(8,128)}, f32[4,6,32,128]{3,2,1,0:T(8,128)S(1)}, u32[]{:S(2)}, u32[]{:S(2)}) collective-permute-start(f32[4,6,32,128]{3,2,1,0:T(8,128)} %param.3), channel_id=1, source_target_pairs={{4,0},{8,4},{12,8},{16,12},{20,16},{24,20},{28,24},{0,28},{5,1},{9... | collective-permute-start | bytes 1179656 | tf_op jit(solution)/shard_map/ppermute | solution.py:25
  20.0 9.5 %copy-start.2 = (f32[6,32,128]{2,1,0:T(8,128)S(1)}, f32[6,32,128]{2,1,0:T(8,128)}, u32[]{:S(2)}) copy-start(f32[6,32,128]{2,1,0:T(8,128)} %param.4) | copy-start | bytes 294916
  33.3 113.2 %reduce-scatter.2.cloned.1.call-start = ((), (), s32[]{:S(2)}) async-start(), calls=%async_computation.2 | async-start | bytes 1966080 | tf_op jit(solution)/shard_map/reduce_scatter | solution.py:56
  85.7 60.8 %copy-start.1 = (f32[4,6,32,128]{3,2,1,0:T(8,128)S(1)}, f32[4,6,32,128]{3,2,1,0:T(8,128)}, u32[]{:S(2)}) copy-start(f32[4,6,32,128]{3,2,1,0:T(8,128)} %fusion.16) | copy-start | bytes 1179652
  106.7 41.6 %copy-start.3 = (f32[128,16]{0,1:T(8,128)}, f32[128,16]{0,1:T(8,128)S(1)}, u32[]{:S(2)}) copy-start(f32[128,16]{0,1:T(8,128)S(1)} %psum.7) | copy-start | bytes 24580
Sparse Core Ops, SparseCore 0:
  33.5 19.7 all-gather.1
  121.3 25.2 reduce-scatter.1
where the time goes:
time: 156 us; the launch traced here: 155 us
  local copies, waits for them, and re-layouts  46.5 us (30%)
  matrix products  33.4 us (21%)
  waiting for transfers between devices  28.2 us (18%)
  blocking collectives  21 us (13%)
  between operations  14.2 us (9%)
  starting transfers between devices  6.41 us (4%)
  other arithmetic  5.59 us (4%)
    reduce_scatter x1, waiting for transfers between devices, shards(): lax.psum_scatter(removed.reshape((col_local * lax.axis_size('band'),) + a...  25.4 us
    psum x1, blocking collectives, shards(): correlation = lax.psum(partial_correlation, 'space')  21 us
    dot_general x1, matrix products, shards(): jnp.einsum('oc,kc->ok', psi_flat, piece.reshape(piece.shape[0], -1), prec...  20.7 us
    unnamed x11, local copies, waits for them, and re-layouts  19 us
    dot_general x2, local copies, waits for them, and re-layouts, shards(): jnp.einsum('ok,oc->kc', correlation, psi_flat, precision=lax.Precision.HI...  14.3 us
    dot_general x1, matrix products, shards(): jnp.einsum('ok,oc->kc', correlation, psi_flat, precision=lax.Precision.HI...  12.7 us
    slice x12, local copies, waits for them, and re-layouts, hamiltonian(): along = along + jnp.roll(values, offset, 3) + jnp.roll(values, -offset, 3)  8.09 us
    slice x12, local copies, waits for them, and re-layouts, hamiltonian(): along = along + jnp.roll(values, offset, 2) + jnp.roll(values, -offset, 2)  5.05 us
  transfers between devices with their start and end apart: 4, of which 3 were waited for; matrix products, arithmetic and copies ran while one was open for 29% of the time, Pallas kernels for 0%

commit v1 on v0

--- a/solution.py
+++ b/solution.py
@@ -51,7 +51,8 @@
     partial_correlation = jnp.einsum(
         "oc,kc->ok", psi_flat, piece.reshape(piece.shape[0], -1), precision=lax.Precision.HIGHEST
     )
-    correlation = lax.psum(partial_correlation, "space")
+    parts = lax.all_gather(partial_correlation, "space")
+    correlation = jnp.sum(parts, axis=0)
     removed = jnp.einsum("ok,oc->kc", correlation, psi_flat, precision=lax.Precision.HIGHEST)
     removed_all = lax.psum_scatter(
         removed.reshape((col_local * lax.axis_size("band"),) + applied.shape[1:]),

time: 156 us -> 167 us (1.071)
  blocking collectives: 21 us -> 30.9 us
  waiting for transfers between devices: 28.2 us -> 31.1 us
  matrix products: 33.4 us -> 31.2 us
    all_gather x0 -> x1, blocking collectives: none -> 30.9 us  [shards(): parts = lax.all_gather(partial_correlation, 'space')]
    psum x1 -> x0, blocking collectives: 21 us -> none  [shards(): correlation = lax.psum(partial_correlation, 'space')]
    reduce_scatter x1, waiting for transfers between devices: 25.4 us -> 28.3 us  [shards(): lax.psum_scatter(removed.reshape((col_local * lax.axis_size('band'),) + a...]
    dot_general x1, matrix products: 12.7 us -> 10.5 us  [shards(): jnp.einsum('ok,oc->kc', correlation, psi_flat, precision=lax.Precision.HI...]
    unnamed x11 -> x14, local copies, waits for them, and re-layouts: 19 us -> 19.1 us
  transfers between devices with their start and end apart: 4 -> 4, of which waited for: 3 -> 3; matrix products, arithmetic and copies ran while one was open for 29% -> 27% of each run, Pallas kernels for 0% -> 0%
where the time goes in v1:
time: 167 us; the launch traced here: 166 us
  local copies, waits for them, and re-layouts  46.5 us (28%)
  matrix products  31.2 us (19%)
  waiting for transfers between devices  31.1 us (19%)
  blocking collectives  30.9 us (19%)
  between operations  14.2 us (9%)
  starting transfers between devices  6.41 us (4%)
  other arithmetic  5.61 us (3%)
    all_gather x1, blocking collectives, shards(): parts = lax.all_gather(partial_correlation, 'space')  30.9 us
    reduce_scatter x1, waiting for transfers between devices, shards(): lax.psum_scatter(removed.reshape((col_local * lax.axis_size('band'),) + a...  28.3 us
    dot_general x1, matrix products, shards(): jnp.einsum('oc,kc->ok', psi_flat, piece.reshape(piece.shape[0], -1), prec...  20.8 us
    unnamed x14, local copies, waits for them, and re-layouts  19.1 us
    dot_general x2, local copies, waits for them, and re-layouts, shards(): jnp.einsum('ok,oc->kc', correlation, psi_flat, precision=lax.Precision.HI...  14.3 us
    dot_general x1, matrix products, shards(): jnp.einsum('ok,oc->kc', correlation, psi_flat, precision=lax.Precision.HI...  10.5 us
    slice x12, local copies, waits for them, and re-layouts, hamiltonian(): along = along + jnp.roll(values, offset, 3) + jnp.roll(values, -offset, 3)  8.09 us
    slice x12, local copies, waits for them, and re-layouts, hamiltonian(): along = along + jnp.roll(values, offset, 2) + jnp.roll(values, -offset, 2)  5.05 us
  transfers between devices with their start and end apart: 4, of which 3 were waited for; matrix products, arithmetic and copies ran while one was open for 27% of the time, Pallas kernels for 0%

profile of v1, /device:TPU:0, one launch (start us, length us, event | category | flops | bytes accessed | tf_op | source)
XLA Modules:
  0.0 166.1 jit_solution(3599535021645321383)
XLA Ops:
  7.2 3.0 %collective-permute-start.1 = (f32[4,6,32,128]{3,2,1,0:T(8,128)}, f32[4,6,32,128]{3,2,1,0:T(8,128)S(1)}, u32[]{:S(2)}, u32[]{:S(2)}) collective-permute-start(f32[4,6,32,128]{3,2,1,0:T(8,128)} %param.3), channel_id=1, source_target_pairs={{0,4},{4,8},{8,12},{12,16},{16,20},{20,24},{24,28},{28,0},{1,5},{5... | collective-permute-start | bytes 1179656 | tf_op jit(solution)/shard_map/ppermute | solution.py:24
  10.3 3.1 %collective-permute-start = (f32[4,6,32,128]{3,2,1,0:T(8,128)}, f32[4,6,32,128]{3,2,1,0:T(8,128)S(1)}, u32[]{:S(2)}, u32[]{:S(2)}) collective-permute-start(f32[4,6,32,128]{3,2,1,0:T(8,128)} %param.3), channel_id=1, source_target_pairs={{4,0},{8,4},{12,8},{16,12},{20,16},{24,20},{28,24},{0,28},{5,1},{9... | collective-permute-start | bytes 1179656 | tf_op jit(solution)/shard_map/ppermute | solution.py:25
  13.4 1.3 fusion.69
  14.6 1.4 fusion.67
  16.0 1.4 fusion.68
  17.4 1.3 fusion.65
  18.6 1.4 fusion.63
  20.0 1.4 fusion.64
  21.4 1.3 fusion.61
  22.6 1.0 fusion.62
  23.6 1.4 fusion.59
  25.0 0.2 fusion.60
  25.2 0.1 fusion.57
  25.3 0.2 fusion.55
  25.4 0.2 fusion.56
  25.7 0.2 fusion.51
  25.9 0.2 fusion.52
  26.2 0.2 fusion.47
  26.4 0.2 fusion.48
  26.6 0.8 collective-permute-done.1
  27.4 0.1 constant_dynamic-update-slice_fusion.1
  27.5 2.0 %collective-permute-done = f32[4,6,32,128]{3,2,1,0:T(8,128)S(1)} collective-permute-done((f32[4,6,32,128]{3,2,1,0:T(8,128)}, f32[4,6,32,128]{3,2,1,0:T(8,128)S(1)}, u32[]{:S(2)}, u32[]{:S(2)}) %collective-permute-start) | collective-permute-done | bytes 393248 | tf_op jit(solution)/shard_map/ppermute | solution.py:25
  29.5 3.8 %fusion.16 = f32[4,6,32,128]{3,2,1,0:T(8,128)} fusion(f32[4,12,32,128]{3,2,1,0:T(8,128)S(1)} %get-tuple-element.53, f32[4,12,32,128]{3,2,1,0:T(8,128)S(1)} %constant_dynamic-update-slice_fusion, f32[4,6,31,128]{3,2,1,0:T(8,128)S(1)} %get-tuple-element.49, f32[4,6,1,128]{3,2,1,0:T(1,128)S(1)} %get-tuple-element.51, ...), kind=kLoop, calls=%fused_computation.14 | loop fusion | flops 6881280 | bytes 15040512 | tf_op jit(solution)/shard_map/add | solution.py:42
  33.3 0.2 reduce-scatter.2.cloned.1.call-start
  33.6 18.9 %copy.79 = f32[16,8,192,128]{3,1,2,0:T(8,128)} copy(f32[16,8,192,128]{3,2,1,0:T(8,128)} %bitcast.26) | data formatting | bytes 25165824
  52.5 12.6 %copy.64 = f32[24576,128]{1,0:T(8,128)} copy(f32[24576,128]{0,1:T(8,128)} %bitcast.28) | data formatting | bytes 25165824 | tf_op jit(solution)/shard_map/ok,oc->kc/dot_general | solution.py:56
  65.1 20.8 %fusion.3 = f32[128,16]{0,1:T(8,128)S(1)} fusion(f32[128,6,32,128]{3,2,1,0:T(8,128)} %param.5, f32[16,6,32,128]{3,2,1,0:T(8,128)} %all-gather.3.cloned.1.call-done), kind=kOutput, calls=%fused_computation.4 | convolution fusion | flops 603979776 | bytes 14163968 | tf_op jit(solution)/shard_map/oc,kc->ok/dot_general | solution.py:51
  85.9 30.9 %all-gather = f32[1024,16]{0,1:T(8,128)S(1)} all-gather(f32[128,16]{0,1:T(8,128)S(1)} %fusion.3), channel_id=2, replica_groups=mesh['space'=8,'band'=4] {'space'}, dimensions={0}, use_global_device_ids=true | all-gather | bytes 73728 | tf_op jit(solution)/shard_map/all_gather | solution.py:54
  116.9 10.5 %fusion.45 = f32[16,6,32,128]{3,0,2,1:T(8,128)S(1)} fusion(f32[6,32,128,128]{3,2,1,0:T(8,128)S(1)} %bitcast.27, f32[128,16]{0,1:T(8,128)S(1)} %bitcast_reduce_fusion), kind=kOutput, calls=%fused_computation.53 | convolution fusion | flops 603979776 | bytes 14163968 | tf_op jit(solution)/shard_map/ok,oc->kc/dot_general | solution.py:56
  127.4 1.7 %copy.65 = f32[16,6,32,128]{3,2,1,0:T(8,128)} copy(f32[16,6,32,128]{3,0,2,1:T(8,128)S(1)} %fusion.45) | data formatting | bytes 3145728 | tf_op jit(solution)/shard_map/ok,oc->kc/dot_general | solution.py:56
  129.1 28.3 %reduce-scatter.2.cloned.1.call-done = f32[4,6,32,128]{3,2,1,0:T(8,128)} async-done(((f32[16,6,32,128]{3,2,1,0:T(8,128)}), f32[4,6,32,128]{3,2,1,0:T(8,128)}) %reduce-scatter.2.cloned.1.call-update) | async-done | bytes 393232 | tf_op jit(solution)/shard_map/reduce_scatter | solution.py:57
  157.4 1.8 %sub.3 = f32[4,6,32,128]{3,2,1,0:T(8,128)} subtract(f32[4,6,32,128]{3,2,1,0:T(8,128)S(1)} %copy-done.2, f32[4,6,32,128]{3,2,1,0:T(8,128)} %reduce-scatter.2.cloned.1.call-done) | non-fusion elementwise | flops 98304 | bytes 1179648 | tf_op jit(solution)/shard_map/sub | solution.py:63
  (25 shorter events, 0.4 us)
Async XLA Ops:
  7.2 17.8 %copy-start = (f32[4,6,32,128]{3,2,1,0:T(8,128)S(1)}, f32[4,6,32,128]{3,2,1,0:T(8,128)}, u32[]{:S(2)}) copy-start(f32[4,6,32,128]{3,2,1,0:T(8,128)} %param.3) | copy-start | bytes 1179652
  7.2 57.9 %all-gather.3.cloned.1.call-start = ((), (), s32[]{:S(2)}) async-start(), calls=%async_computation.1 | async-start | bytes 1966080 | tf_op jit(solution)/shard_map/all_gather | solution.py:50
  7.2 20.2 %collective-permute-start.1 = (f32[4,6,32,128]{3,2,1,0:T(8,128)}, f32[4,6,32,128]{3,2,1,0:T(8,128)S(1)}, u32[]{:S(2)}, u32[]{:S(2)}) collective-permute-start(f32[4,6,32,128]{3,2,1,0:T(8,128)} %param.3), channel_id=1, source_target_pairs={{0,4},{4,8},{8,12},{12,16},{16,20},{20,24},{24,28},{28,0},{1,5},{5... | collective-permute-start | bytes 1179656 | tf_op jit(solution)/shard_map/ppermute | solution.py:24
  10.3 19.2 %collective-permute-start = (f32[4,6,32,128]{3,2,1,0:T(8,128)}, f32[4,6,32,128]{3,2,1,0:T(8,128)S(1)}, u32[]{:S(2)}, u32[]{:S(2)}) collective-permute-start(f32[4,6,32,128]{3,2,1,0:T(8,128)} %param.3), channel_id=1, source_target_pairs={{4,0},{8,4},{12,8},{16,12},{20,16},{24,20},{28,24},{0,28},{5,1},{9... | collective-permute-start | bytes 1179656 | tf_op jit(solution)/shard_map/ppermute | solution.py:25
  20.0 9.5 %copy-start.3 = (f32[6,32,128]{2,1,0:T(8,128)S(1)}, f32[6,32,128]{2,1,0:T(8,128)}, u32[]{:S(2)}) copy-start(f32[6,32,128]{2,1,0:T(8,128)} %param.4) | copy-start | bytes 294916
  33.3 124.1 %reduce-scatter.2.cloned.1.call-start = ((), (), s32[]{:S(2)}) async-start(), calls=%async_computation.2 | async-start | bytes 1966080 | tf_op jit(solution)/shard_map/reduce_scatter | solution.py:57
  65.1 51.8 %copy-start.1 = (f32[24576,128]{1,0:T(8,128)S(1)}, f32[24576,128]{1,0:T(8,128)}, u32[]{:S(2)}) copy-start(f32[24576,128]{1,0:T(8,128)} %copy.64) | copy-start | bytes 37748740
  85.9 71.5 %copy-start.2 = (f32[4,6,32,128]{3,2,1,0:T(8,128)S(1)}, f32[4,6,32,128]{3,2,1,0:T(8,128)}, u32[]{:S(2)}) copy-start(f32[4,6,32,128]{3,2,1,0:T(8,128)} %fusion.16) | copy-start | bytes 1179652
  116.9 42.3 %copy-start.4 = (f32[128,16]{0,1:T(8,128)}, f32[128,16]{0,1:T(8,128)S(1)}, u32[]{:S(2)}) copy-start(f32[128,16]{0,1:T(8,128)S(1)} %bitcast_reduce_fusion) | copy-start | bytes 24580
Sparse Core Ops, SparseCore 0:
  33.5 19.7 all-gather.2
  129.2 28.1 reduce-scatter.1
